TPU v7x, 128 devices: a whole 4x4x4 slice. The times are simulated.
128 devices in a mesh: rel: 4 (over z), ent: 32 (over y, x, core).
Axes of the slice: x: 4, y: 4, z: 4, core: 2. Of those that a mesh axis runs over, the one named last changes fastest.
Arguments:
- features: bfloat16 [16384, 512], P('ent'), may hold values from -6 to 6
- w_self: bfloat16 [512, 512], replicated, may hold values from -0.25 to 0.25
- basis_mats: bfloat16 [16384, 512], replicated, may hold values from -0.046875 to 0.046875
- basis_coeffs: float32 [1000, 32], replicated, may hold values from -5 to 5
- group_rels: int32 [1000], P('rel'), may hold values from 0 to 999, each once
- rel_local: int32 [65536], P(('rel', 'ent')), may hold values from 0 to 249
- edge_src: int32 [65536], P(('rel', 'ent')), may hold values from 0 to 16383, as said below
- edge_dst: int32 [65536], P(('rel', 'ent')), may hold values from 0 to 16383, as said below
- block_counts: int32 [4, 32, 32], P('rel', 'ent'), may hold values from 1 to 16, as said below
- cotangent: bfloat16 [16384, 512], P('ent'), may hold values from -6 to 6
Outputs:
- activations: bfloat16 [16384, 512], P('ent')
- grad_features: bfloat16 [16384, 512], P('ent')
- grad_basis: float32 [16384, 512], P(('rel', 'ent'))
Inputs may be any that keep to these rules, and one draw needn't show every extreme that they name: `edge_src`: slot i's source is owned by ent index (i // 512) % 32: it lies in [that index * 512, that index * 512 + 512). `edge_dst`: slot i's destination is owned by block index k = (i % 512) // 16: it lies in [k * 512, k * 512 + 512); within each aligned block of 16 slots the destinations are non-decreasing; the live slots of a block are its first block_counts ones. `block_counts`: one relation group, drawn from the seed, has every block full.
All inputs are finite; a program needn't handle non-finite values.
Results may differ from a plain program's by a relative error of at most 0.0059.
Values may be sent and summed in bfloat16 or wider, within the bound.
A program may use at most 192 MiB of HBM per device.

v0:
```python
import jax
import jax.numpy as jnp
from jax import lax
from jax.sharding import PartitionSpec as P

BF = jnp.bfloat16
F32 = jnp.float32


def dot(a, b, dims=((1,), (0,)), precision=None):
    return lax.dot_general(a, b, (dims, ((), ())), preferred_element_type=F32, precision=precision)


def swap(x, axis):
    return lax.all_to_all(x, axis, split_axis=0, concat_axis=0, tiled=True)


def per_device(
    features,
    w_self,
    basis_mats,
    basis_coeffs,
    group_rels,
    rel_local,
    edge_src,
    edge_dst,
    block_counts,
    cotangent,
):
    n_ent, width = features.shape
    ent_count = lax.axis_size("ent")
    rel_count = lax.axis_size("rel")
    slots = rel_local.shape[0]
    cap = slots // ent_count
    bases = basis_coeffs.shape[1]
    rels = basis_coeffs.shape[0]
    part = width // rel_count
    q = lax.axis_index("rel")
    s = lax.axis_index("ent")
    all_slots = slots * rel_count
    pos = jnp.arange(slots, dtype=jnp.int32)
    limits = jnp.repeat(block_counts.reshape(ent_count), cap, total_repeat_length=slots)
    live = pos % cap < limits
    src_own = edge_src - s * n_ent
    dst_own = jnp.where(live, edge_dst - pos // cap * n_ent, n_ent)
    rel_own = group_rels[rel_local]
    meta = jnp.stack([src_own, dst_own, rel_own])
    meta = lax.all_gather(meta, "rel").reshape(rel_count, 3, ent_count, cap)
    meta = meta.transpose(2, 1, 0, 3)
    src = meta[:, 0].reshape(all_slots)
    arrived = swap(meta[:, 1:], "ent")
    dst = arrived[:, 0].reshape(all_slots)
    rel = arrived[:, 1].reshape(all_slots)
    ids = jnp.arange(n_ent, dtype=jnp.int32)[:, None]
    pick_src = (ids == src[None, :]).astype(BF)
    feat_part = lax.dynamic_slice_in_dim(features, q * part, part, 1)
    rows = dot(pick_src, feat_part, ((0,), (0,))).astype(BF)
    rows = swap(rows.reshape(ent_count, rel_count * cap, part), "ent").reshape(all_slots, part)
    pick_rel = (jnp.arange(rels, dtype=jnp.int32)[:, None] == rel[None, :]).astype(F32)
    coef_t = dot(basis_coeffs, pick_rel, ((0,), (0,)), lax.Precision.HIGHEST)
    pick = (ids == dst[None, :]).astype(BF)
    degree = jnp.sum(pick, axis=1, dtype=F32)
    inverse = (1.0 / jnp.maximum(degree, 1.0))[:, None]
    mixed_t = (
        (coef_t[:, None, :] * rows.T.astype(F32)[None]).reshape(bases * part, all_slots).astype(BF)
    )
    agg = dot(pick, mixed_t, ((1,), (1,))).astype(BF)
    basis_part = lax.dynamic_slice_in_dim(
        basis_mats.reshape(bases, width, width), q * part, part, 1
    ).reshape(bases * part, width)
    partial = dot(agg, basis_part).astype(BF)
    partial = swap(partial.reshape(n_ent, rel_count, part).transpose(1, 0, 2), "rel")
    sums = jnp.sum(partial.astype(F32), axis=0)
    w_part = lax.dynamic_slice_in_dim(w_self, q * part, part, 1)
    cot = lax.dynamic_slice_in_dim(cotangent, q * part, part, 1).astype(F32)
    pre = dot(features, w_part) + sums * inverse
    sig = jax.nn.sigmoid(pre)
    act = (pre * sig).astype(BF)
    grad_pre = (cot * (sig * (1.0 + pre * (1.0 - sig)))).astype(BF)
    act = lax.all_gather(act, "rel", axis=1, tiled=True)
    grad_pre = lax.all_gather(grad_pre, "rel", axis=1, tiled=True)
    scaled = (grad_pre.astype(F32) * inverse).astype(BF)
    basis_terms = dot(agg, scaled, ((0,), (0,))).astype(BF)
    basis_terms = swap(basis_terms.reshape(ent_count, part, width), "ent")
    block = jnp.sum(basis_terms.astype(F32), axis=0)
    per_rel = bases // rel_count
    routes = [
        (r * ent_count + b, b // per_rel * ent_count + b % per_rel * rel_count + r)
        for r in range(rel_count)
        for b in range(bases)
    ]
    grad_basis = lax.ppermute(block, ("rel", "ent"), routes)
    back_t = dot(basis_part, scaled, ((1,), (1,))).astype(BF)
    spread = dot(back_t, pick).reshape(bases, part, all_slots)
    grad_rows = jnp.sum(spread * coef_t[:, None, :], axis=0).astype(BF).T
    grad_rows = swap(grad_rows.reshape(ent_count, rel_count * cap, part), "ent")
    w_rows = lax.dynamic_slice_in_dim(w_self, q * part, part, 0)
    grad_part = dot(grad_pre, w_rows, ((1,), (1,))) + dot(
        pick_src, grad_rows.reshape(all_slots, part)
    )
    grad_features = lax.all_gather(grad_part.astype(BF), "rel", axis=1, tiled=True)
    return (act, grad_features, grad_basis)


def solution(mesh):
    placed = (
        P("ent", None),
        P(),
        P(),
        P(),
        P("rel"),
        P(("rel", "ent")),
        P(("rel", "ent")),
        P(("rel", "ent")),
        P("rel", "ent", None),
        P("ent", None),
    )
    return jax.shard_map(
        per_device,
        mesh=mesh,
        in_specs=placed,
        out_specs=(P("ent", None), P("ent", None), P(("rel", "ent"), None)),
        check_vma=False,
    )
```

profile of v0, /device:TPU:27, one launch (start us, length us, event | category | flops | bytes accessed | tf_op | source)
XLA Modules:
  0.0 229.3 jit_solution(15646126451064702323)
XLA Ops:
  6.0 4.5 %compare_select_fusion.1 = (s32[512,1]{0,1:T(1,128)S(1)}, s32[512,1]{0,1:T(1,128)S(1)}) fusion(s32[]{:T(128)} %bitcast.31, s32[]{:T(128)} %bitcast.32, s32[]{:T(128)} %bitcast.33, s32[]{:T(128)} %bitcast.34, s32[]{:T(128)} %bitcast.35, s32[]{:T(128)} %bitcast.37, s32[]{:T(128)} %bitcast.36, s32[512,1]{0,1:T(1,128)S(1)} %bitcast.106, s32[512,1]{0,1:T(1,128)S(1)} %bitcast.105), kind=kLoop, calls=%fused_computation.66 | loop fusion | flops 7168 | bytes 8220 | tf_op jit(solution)/shard_map/jit(_take)/gather | solution.py:42
  11.4 3.6 %gather_fusion = s32[512]{0:T(512)S(1)} fusion(s32[250]{0:T(256)} %param.16, s32[1024]{0:T(1024)S(1)} %pad_clamp_fusion), kind=kCustom, calls=%fused_computation | custom fusion | bytes 6144 | tf_op jit(solution)/shard_map/gather | solution.py:46
  15.0 16.4 %fusion.23 = s32[512]{0:T(512)S(1)} fusion(s32[512]{0:T(512)} %param.19, pred[512]{0:T(512)(128)(4,1)S(1)} %get-tuple-element.51, pred[512]{0:T(512)(128)(4,1)S(1)} %get-tuple-element.50, pred[512]{0:T(512)(128)(4,1)S(1)} %get-tuple-element.49, pred[512]{0:T(512)(128)(4,1)S(1)} %get-tuple-element.48, pred[512]{0:T(512)(128)(4,1)S(1)} %get-tuple-element.47, ...), kind=kLoop, calls=%fused_computation.85 | loop fusion | flops 25600 | bytes 21108 | tf_op jit(solution)/shard_map/jit(_where)/select_n | solution.py:45
  31.4 10.5 %all-gather.1 = s32[4,3,512]{2,1,0:T(4,128)S(1)} all-gather(s32[1,3,512]{2,1,0:T(4,128)S(1)} %add_bitcast_fusion), channel_id=2, replica_groups=mesh['rel'=4,'ent'=32] {'rel'}, dimensions={0}, use_global_device_ids=true | all-gather | bytes 30720 | tf_op jit(solution)/shard_map/all_gather | solution.py:48
  42.9 10.3 %all-to-all-start = ((s32[32,1,128]{2,1,0:T(1,128)}), s32[32,1,128]{2,1,0:T(1,128)S(1)}, u32[]{:S(2)}, u32[]{:S(2)}) async-start(s32[32,1,128]{2,1,0:T(1,128)} %reshape.365), calls=%async_computation | async-start | bytes 32768 | tf_op jit(solution)/shard_map/all_to_all | solution.py:15
  57.3 7.0 %all-to-all-start.1 = ((bf16[32,64,128]{2,1,0:T(8,128)(2,1)}), bf16[32,64,128]{2,1,0:T(8,128)(2,1)S(1)}, u32[]{:S(2)}, u32[]{:S(2)}) async-start(bf16[32,64,128]{2,1,0:T(8,128)(2,1)} %bitcast.44), calls=%async_computation.1 | async-start | bytes 1048576 | tf_op jit(solution)/shard_map/all_to_all | solution.py:15
  64.3 4.6 %constant_dynamic-slice_fusion.1 = bf16[32,128,512]{2,1,0:T(8,128)(2,1)} fusion(bf16[32,512,512]{2,1,0:T(8,128)(2,1)} %bitcast.98, s32[]{:T(128)S(6)} %select_n.47), kind=kLoop, calls=%fused_computation.95 | loop fusion | bytes 8388612 | tf_op jit(solution)/shard_map/dynamic_slice | solution.py:68
  70.5 3.0 %fusion.7 = f32[32,2048]{1,0:T(8,128)S(1)} fusion(f32[1000,32]{0,1:T(8,128)S(1)} %copy-done.4, s32[2048]{0:T(1024)S(1)} %eq.52), kind=kOutput, calls=%fused_computation.18 | convolution fusion | flops 788480000 | bytes 398336 | tf_op jit(solution)/shard_map/dot_general | solution.py:11
  73.9 6.8 %multiply_convert_fusion = bf16[32,128,2048]{2,1,0:T(8,128)(2,1)} fusion(f32[128,2048]{1,0:T(8,128)S(1)} %bitcast.93, f32[32,2048]{1,0:T(8,128)S(1)} %fusion.7), kind=kLoop, calls=%fused_computation.2 | loop fusion | flops 16777216 | bytes 18087936 | tf_op jit(solution)/shard_map/convert_element_type | solution.py:65
  80.8 13.9 %convolution_convert_fusion = bf16[512,4096]{1,0:T(8,128)(2,1)} fusion(bf16[4096,2048]{1,0:T(8,128)(2,1)} %bitcast.92, s32[2048]{0:T(1024)S(1)} %eq.48), kind=kOutput, calls=%fused_computation.6 | convolution fusion | flops 8593080320 | bytes 20979712 | tf_op jit(solution)/shard_map/dot_general | solution.py:11
  94.7 5.5 %convolution_convert_fusion.3 = bf16[512,512]{0,1:T(8,128)(2,1)} fusion(bf16[512,4096]{1,0:T(8,128)(2,1)} %convolution_convert_fusion, bf16[4096,512]{1,0:T(8,128)(2,1)S(1)} %bitcast.95), kind=kOutput, calls=%fused_computation.23 | convolution fusion | flops 2147745792 | bytes 8912896 | tf_op jit(solution)/shard_map/dot_general | solution.py:11
  100.1 3.8 %all-to-all-start.2 = ((bf16[4,512,128]{1,2,0:T(8,128)(2,1)}), bf16[4,512,128]{1,2,0:T(8,128)(2,1)S(1)}, u32[]{:S(2)}, u32[]{:S(2)}) async-start(bf16[4,512,128]{1,2,0:T(8,128)(2,1)} %bitcast.51), calls=%async_computation.2 | async-start | bytes 1048576 | tf_op jit(solution)/shard_map/all_to_all | solution.py:15
  105.5 7.4 %all-to-all-done.2 = bf16[4,512,128]{1,2,0:T(8,128)(2,1)S(1)} async-done(((bf16[4,512,128]{1,2,0:T(8,128)(2,1)}), bf16[4,512,128]{1,2,0:T(8,128)(2,1)S(1)}, u32[]{:S(2)}, u32[]{:S(2)}) %all-to-all-start.2) | async-done | bytes 524320 | tf_op jit(solution)/shard_map/all_to_all | solution.py:15
  113.4 10.7 %all_gather.18 = bf16[512,512]{0,1:T(8,128)(2,1)S(1)} all-gather(bf16[512,128]{0,1:T(8,128)(2,1)S(1)} %get-tuple-element.54), channel_id=1, replica_groups=mesh['rel'=4,'ent'=32] {'rel'}, dimensions={1}, use_global_device_ids=true | all-gather | bytes 655360 | tf_op jit(solution)/shard_map/all_gather | solution.py:81
  124.1 6.6 %convolution_convert_fusion.1 = bf16[4096,512]{1,0:T(8,128)(2,1)} fusion(bf16[512,4096]{1,0:T(8,128)(2,1)} %convolution_convert_fusion, bf16[512,512]{0,1:T(8,128)(2,1)S(1)} %all_gather.18, f32[512]{0:T(512)S(1)} %maximum_divide_fusion), kind=kOutput, calls=%fused_computation.7 | convolution fusion | flops 2150367232 | bytes 8914944 | tf_op jit(solution)/shard_map/dot_general | solution.py:11
  130.8 11.3 %all-to-all-start.4 = ((bf16[32,128,512]{2,1,0:T(8,128)(2,1)}), bf16[32,128,512]{2,1,0:T(8,128)(2,1)}, u32[]{:S(2)}, u32[]{:S(2)}) async-start(bf16[32,128,512]{2,1,0:T(8,128)(2,1)} %bitcast.96), calls=%async_computation.4 | async-start | bytes 8388608 | tf_op jit(solution)/shard_map/all_to_all | solution.py:15
  142.1 11.1 %all_gather.17 = bf16[512,512]{0,1:T(8,128)(2,1)S(1)} all-gather(bf16[512,128]{0,1:T(8,128)(2,1)S(1)} %get-tuple-element.55), channel_id=1, replica_groups=mesh['rel'=4,'ent'=32] {'rel'}, dimensions={1}, use_global_device_ids=true | all-gather | bytes 655360 | tf_op jit(solution)/shard_map/all_gather | solution.py:80
  154.2 4.5 %convolution_convert_fusion.2.clone.5 = bf16[4096,512]{1,0:T(8,128)(2,1)S(1)} fusion(bf16[4096,512]{1,0:T(8,128)(2,1)} %bitcast.94, bf16[512,512]{0,1:T(8,128)(2,1)S(1)} %all_gather.18, f32[512]{0:T(512)S(1)} %maximum_divide_fusion), kind=kOutput, calls=%fused_computation.8.clone.clone.clone.2 | convolution fusion | flops 2150367232 | bytes 8914944 | tf_op jit(solution)/shard_map/dot_general | solution.py:11
  158.7 14.6 %fusion.3 = f32[4096,2048]{1,0:T(8,128)} fusion(s32[2048]{0:T(1024)S(1)} %eq.48, bf16[4096,512]{1,0:T(8,128)(2,1)S(1)} %convolution_convert_fusion.2.clone.5), kind=kOutput, calls=%fused_computation.14 | convolution fusion | flops 8590983168 | bytes 37756928 | tf_op jit(solution)/shard_map/dot_general | solution.py:11
  173.3 12.5 %multiply_reduce_fusion = bf16[128,2048]{1,0:T(8,128)(2,1)S(1)} fusion(f32[32,128,2048]{2,1,0:T(8,128)} %bitcast.91, f32[32,2048]{1,0:T(8,128)S(1)} %fusion.7), kind=kLoop, calls=%fused_computation.1 | loop fusion | flops 16515072 | bytes 34340864 | tf_op jit(solution)/shard_map/reduce_sum | solution.py:95
  186.8 5.1 %all-to-all-done.4 = bf16[32,128,512]{2,1,0:T(8,128)(2,1)} async-done(((bf16[32,128,512]{2,1,0:T(8,128)(2,1)}), bf16[32,128,512]{2,1,0:T(8,128)(2,1)}, u32[]{:S(2)}, u32[]{:S(2)}) %all-to-all-start.4) | async-done | bytes 4194336 | tf_op jit(solution)/shard_map/all_to_all | solution.py:15
  191.9 7.6 %all-to-all-start.3 = ((bf16[32,64,128]{2,1,0:T(8,128)(2,1)}), bf16[32,64,128]{2,1,0:T(8,128)(2,1)S(1)}, u32[]{:S(2)}, u32[]{:S(2)}) async-start(bf16[32,64,128]{2,1,0:T(8,128)(2,1)} %bitcast.54), calls=%async_computation.3 | async-start | bytes 1048576 | tf_op jit(solution)/shard_map/all_to_all | solution.py:15
  202.7 4.7 %collective-permute-start = (f32[128,512]{1,0:T(8,128)S(1)}, f32[128,512]{1,0:T(8,128)S(1)}, u32[]{:S(2)}, u32[]{:S(2)}) collective-permute-start(f32[128,512]{1,0:T(8,128)S(1)} %convert_reduce_fusion), channel_id=1, source_target_pairs={{0,0},{1,4},{2,8},{3,12},{4,16},{5,20},{6,24},{7,28},{8,32},{9,36}... | collective-permute-start | bytes 786440 | tf_op jit(solution)/shard_map/ppermute | solution.py:92
  209.5 18.3 %all_gather.19 = bf16[512,512]{1,0:T(8,128)(2,1)S(1)} all-gather(bf16[512,128]{1,0:T(8,128)(2,1)S(1)} %fusion.14), channel_id=1, replica_groups=mesh['rel'=4,'ent'=32] {'rel'}, dimensions={1}, use_global_device_ids=true | all-gather | bytes 655360 | tf_op jit(solution)/shard_map/all_gather | solution.py:101
  (53 shorter events, 24.1 us)
Async XLA Ops:
  0.6 52.7 %copy-start = (bf16[512,512]{1,0:T(8,128)(2,1)S(1)}, bf16[512,512]{1,0:T(8,128)(2,1)}, u32[]{:S(2)}) copy-start(bf16[512,512]{1,0:T(8,128)(2,1)} %param.12) | copy-start | bytes 1572868
  42.9 14.5 %all-to-all-start = ((s32[32,1,128]{2,1,0:T(1,128)}), s32[32,1,128]{2,1,0:T(1,128)S(1)}, u32[]{:S(2)}, u32[]{:S(2)}) async-start(s32[32,1,128]{2,1,0:T(1,128)} %reshape.365), calls=%async_computation | async-start | bytes 32768 | tf_op jit(solution)/shard_map/all_to_all | solution.py:15
  57.3 16.1 %all-to-all-start.1 = ((bf16[32,64,128]{2,1,0:T(8,128)(2,1)}), bf16[32,64,128]{2,1,0:T(8,128)(2,1)S(1)}, u32[]{:S(2)}, u32[]{:S(2)}) async-start(bf16[32,64,128]{2,1,0:T(8,128)(2,1)} %bitcast.44), calls=%async_computation.1 | async-start | bytes 1048576 | tf_op jit(solution)/shard_map/all_to_all | solution.py:15
  64.3 6.2 %copy-start.4 = (f32[1000,32]{0,1:T(8,128)S(1)}, f32[1000,32]{0,1:T(8,128)}, u32[]{:S(2)}) copy-start(f32[1000,32]{0,1:T(8,128)} %param.15) | copy-start | bytes 384004
  80.7 13.9 %copy-start.2 = (bf16[32,128,512]{2,1,0:T(8,128)(2,1)S(1)}, bf16[32,128,512]{2,1,0:T(8,128)(2,1)}, u32[]{:S(2)}) copy-start(bf16[32,128,512]{2,1,0:T(8,128)(2,1)} %constant_dynamic-slice_fusion.1) | copy-start | bytes 12582916
  94.7 18.3 %copy-start.3 = (bf16[512,512]{1,0:T(8,128)(2,1)S(1)}, bf16[512,512]{1,0:T(8,128)(2,1)}, u32[]{:S(2)}) copy-start(bf16[512,512]{1,0:T(8,128)(2,1)} %param.13) | copy-start | bytes 1572868
  100.1 12.8 %all-to-all-start.2 = ((bf16[4,512,128]{1,2,0:T(8,128)(2,1)}), bf16[4,512,128]{1,2,0:T(8,128)(2,1)S(1)}, u32[]{:S(2)}, u32[]{:S(2)}) async-start(bf16[4,512,128]{1,2,0:T(8,128)(2,1)} %bitcast.51), calls=%async_computation.2 | async-start | bytes 1048576 | tf_op jit(solution)/shard_map/all_to_all | solution.py:15
  130.8 61.1 %all-to-all-start.4 = ((bf16[32,128,512]{2,1,0:T(8,128)(2,1)}), bf16[32,128,512]{2,1,0:T(8,128)(2,1)}, u32[]{:S(2)}, u32[]{:S(2)}) async-start(bf16[32,128,512]{2,1,0:T(8,128)(2,1)} %bitcast.96), calls=%async_computation.4 | async-start | bytes 8388608 | tf_op jit(solution)/shard_map/all_to_all | solution.py:15
  191.9 16.7 %all-to-all-start.3 = ((bf16[32,64,128]{2,1,0:T(8,128)(2,1)}), bf16[32,64,128]{2,1,0:T(8,128)(2,1)S(1)}, u32[]{:S(2)}, u32[]{:S(2)}) async-start(bf16[32,64,128]{2,1,0:T(8,128)(2,1)} %bitcast.54), calls=%async_computation.3 | async-start | bytes 1048576 | tf_op jit(solution)/shard_map/all_to_all | solution.py:15
  199.5 29.8 %copy-start.1 = (bf16[512,512]{1,0:T(8,128)(2,1)S(1)}, bf16[512,512]{1,0:T(8,128)(2,1)}, u32[]{:S(2)}) copy-start(bf16[512,512]{1,0:T(8,128)(2,1)} %param.12) | copy-start | bytes 1572868
  202.7 25.1 %collective-permute-start = (f32[128,512]{1,0:T(8,128)S(1)}, f32[128,512]{1,0:T(8,128)S(1)}, u32[]{:S(2)}, u32[]{:S(2)}) collective-permute-start(f32[128,512]{1,0:T(8,128)S(1)} %convert_reduce_fusion), channel_id=1, source_target_pairs={{0,0},{1,4},{2,8},{3,12},{4,16},{5,20},{6,24},{7,28},{8,32},{9,36}... | collective-permute-start | bytes 786440 | tf_op jit(solution)/shard_map/ppermute | solution.py:92
where the time goes:
time: 230 us; the launch traced here: 229 us
  matrix products  51.8 us (23%)
  blocking collectives  50.6 us (22%)
  other arithmetic  46.6 us (20%)
  starting transfers between devices  44.7 us (19%)
  local copies, waits for them, and re-layouts  19 us (8%)
  waiting for transfers between devices  15.7 us (7%)
    dot_general x10, matrix products, dot(): lax.dot_general(a, b, (dims, ((), ())), preferred_element_type=F32, preci...  51.8 us
    all_to_all x5, starting transfers between devices, swap(): return lax.all_to_all(x, axis, split_axis=0, concat_axis=0, tiled=True)  40 us
    all_gather x1, blocking collectives, per_device(): lax.all_gather(grad_part.astype(BF), 'rel', axis=1, tiled=True)  18.3 us
    select_n x1, other arithmetic, per_device(): dst_own = jnp.where(live, edge_dst - pos // cap * n_ent, n_ent)  16.4 us
    all_to_all x5, waiting for transfers between devices, swap(): return lax.all_to_all(x, axis, split_axis=0, concat_axis=0, tiled=True)  15.7 us
    reduce_sum x1, other arithmetic, per_device(): grad_rows = jnp.sum(spread * coef_t[:, None, :], axis=0).astype(BF).T  12.5 us
    all_gather x1, blocking collectives, per_device(): act = lax.all_gather(act, 'rel', axis=1, tiled=True)  11.1 us
    all_gather x1, blocking collectives, per_device(): grad_pre = lax.all_gather(grad_pre, 'rel', axis=1, tiled=True)  10.7 us
  transfers between devices with their start and end apart: 6, of which 4 were waited for; matrix products, arithmetic and copies ran while one was open for 22% of the time, Pallas kernels for 0%

commit v1 on v0

--- a/solution.py
+++ b/solution.py
@@ -5,6 +5,14 @@
 
 BF = jnp.bfloat16
 F32 = jnp.float32
+
+
+def gather_by_exchange(shard, axis, dim):
+    length = lax.axis_size(axis)
+    repeats = [length if d == dim else 1 for d in range(shard.ndim)]
+    return lax.all_to_all(
+        jnp.tile(shard, repeats), axis, split_axis=dim, concat_axis=dim, tiled=True
+    )
 
 
 def dot(a, b, dims=((1,), (0,)), precision=None):
@@ -98,7 +106,7 @@
     grad_part = dot(grad_pre, w_rows, ((1,), (1,))) + dot(
         pick_src, grad_rows.reshape(all_slots, part)
     )
-    grad_features = lax.all_gather(grad_part.astype(BF), "rel", axis=1, tiled=True)
+    grad_features = gather_by_exchange(grad_part.astype(BF), "rel", 1)
     return (act, grad_features, grad_basis)
 
 

time: 230 us -> 270 us (1.17)
  the two profiles are of different devices: /device:TPU:27 before, /device:TPU:26 now
where the time goes in v1:
time: 270 us; the launch traced here: 269 us
  waiting for transfers between devices  61.5 us (23%)
  matrix products  51.7 us (19%)
  other arithmetic  46.7 us (17%)
  blocking collectives  44.5 us (16%)
  starting transfers between devices  43.3 us (16%)
  local copies, waits for them, and re-layouts  20.3 us (8%)
    all_to_all x5, waiting for transfers between devices, swap(): return lax.all_to_all(x, axis, split_axis=0, concat_axis=0, tiled=True)  61.5 us
    dot_general x10, matrix products, dot(): lax.dot_general(a, b, (dims, ((), ())), preferred_element_type=F32, preci...  51.7 us
    all_to_all x5, starting transfers between devices, swap(): return lax.all_to_all(x, axis, split_axis=0, concat_axis=0, tiled=True)  33.5 us
    all_gather x1, blocking collectives, per_device(): act = lax.all_gather(act, 'rel', axis=1, tiled=True)  17.9 us
    select_n x1, other arithmetic, per_device(): dst_own = jnp.where(live, edge_dst - pos // cap * n_ent, n_ent)  16.4 us
    all_gather x1, blocking collectives, per_device(): grad_pre = lax.all_gather(grad_pre, 'rel', axis=1, tiled=True)  13.4 us
    all_gather x1, blocking collectives, per_device(): meta = lax.all_gather(meta, 'rel').reshape(rel_count, 3, ent_count, cap)  13.1 us
    reduce_sum x1, other arithmetic, per_device(): grad_rows = jnp.sum(spread * coef_t[:, None, :], axis=0).astype(BF).T  12.5 us
  transfers between devices with their start and end apart: 7, of which 4 were waited for; matrix products, arithmetic and copies ran while one was open for 10% of the time, Pallas kernels for 0%

profile of v1, /device:TPU:26, one launch (start us, length us, event | category | flops | bytes accessed | tf_op | source)
XLA Modules:
  0.0 268.9 jit_solution(2613591434929838107)
XLA Ops:
  6.0 4.5 %compare_select_fusion.1 = (s32[512,1]{0,1:T(1,128)S(1)}, s32[512,1]{0,1:T(1,128)S(1)}) fusion(s32[]{:T(128)} %bitcast.31, s32[]{:T(128)} %bitcast.32, s32[]{:T(128)} %bitcast.33, s32[]{:T(128)} %bitcast.34, s32[]{:T(128)} %bitcast.35, s32[]{:T(128)} %bitcast.37, s32[]{:T(128)} %bitcast.36, s32[512,1]{0,1:T(1,128)S(1)} %bitcast.108, s32[512,1]{0,1:T(1,128)S(1)} %bitcast.107), kind=kLoop, calls=%fused_computation.66 | loop fusion | flops 7168 | bytes 8220 | tf_op jit(solution)/shard_map/jit(_take)/gather | solution.py:50
  11.4 3.6 %gather_fusion = s32[512]{0:T(512)S(1)} fusion(s32[250]{0:T(256)} %param.16, s32[1024]{0:T(1024)S(1)} %pad_clamp_fusion), kind=kCustom, calls=%fused_computation | custom fusion | bytes 6144 | tf_op jit(solution)/shard_map/gather | solution.py:54
  15.0 16.4 %fusion.23 = s32[512]{0:T(512)S(1)} fusion(s32[512]{0:T(512)} %param.19, pred[512]{0:T(512)(128)(4,1)S(1)} %get-tuple-element.54, pred[512]{0:T(512)(128)(4,1)S(1)} %get-tuple-element.53, pred[512]{0:T(512)(128)(4,1)S(1)} %get-tuple-element.52, pred[512]{0:T(512)(128)(4,1)S(1)} %get-tuple-element.51, pred[512]{0:T(512)(128)(4,1)S(1)} %get-tuple-element.50, ...), kind=kLoop, calls=%fused_computation.85 | loop fusion | flops 25600 | bytes 21108 | tf_op jit(solution)/shard_map/jit(_where)/select_n | solution.py:53
  31.4 13.1 %all-gather.1 = s32[4,3,512]{2,1,0:T(4,128)S(1)} all-gather(s32[1,3,512]{2,1,0:T(4,128)S(1)} %add_bitcast_fusion), channel_id=2, replica_groups=mesh['rel'=4,'ent'=32] {'rel'}, dimensions={0}, use_global_device_ids=true | all-gather | bytes 30720 | tf_op jit(solution)/shard_map/all_gather | solution.py:56
  45.5 7.3 %all-to-all-start = ((s32[32,1,128]{2,1,0:T(1,128)}), s32[32,1,128]{2,1,0:T(1,128)S(1)}, u32[]{:S(2)}, u32[]{:S(2)}) async-start(s32[32,1,128]{2,1,0:T(1,128)} %reshape.372), calls=%async_computation | async-start | bytes 32768 | tf_op jit(solution)/shard_map/all_to_all | solution.py:23
  57.3 6.7 %all-to-all-start.1 = ((bf16[32,64,128]{2,1,0:T(8,128)(2,1)}), bf16[32,64,128]{2,1,0:T(8,128)(2,1)S(1)}, u32[]{:S(2)}, u32[]{:S(2)}) async-start(bf16[32,64,128]{2,1,0:T(8,128)(2,1)} %bitcast.44), calls=%async_computation.1 | async-start | bytes 1048576 | tf_op jit(solution)/shard_map/all_to_all | solution.py:23
  64.0 4.6 %constant_dynamic-slice_fusion.1 = bf16[32,128,512]{2,1,0:T(8,128)(2,1)} fusion(bf16[32,512,512]{2,1,0:T(8,128)(2,1)} %bitcast.100, s32[]{:T(128)S(6)} %select_n.47), kind=kLoop, calls=%fused_computation.95 | loop fusion | bytes 8388612 | tf_op jit(solution)/shard_map/dynamic_slice | solution.py:76
  70.2 3.0 %fusion.7 = f32[32,2048]{1,0:T(8,128)S(1)} fusion(f32[1000,32]{0,1:T(8,128)S(1)} %copy-done.4, s32[2048]{0:T(1024)S(1)} %eq.52), kind=kOutput, calls=%fused_computation.18 | convolution fusion | flops 788480000 | bytes 398336 | tf_op jit(solution)/shard_map/dot_general | solution.py:19
  73.6 6.8 %multiply_convert_fusion = bf16[32,128,2048]{2,1,0:T(8,128)(2,1)} fusion(f32[128,2048]{1,0:T(8,128)S(1)} %bitcast.94, f32[32,2048]{1,0:T(8,128)S(1)} %fusion.7), kind=kLoop, calls=%fused_computation.2 | loop fusion | flops 16777216 | bytes 18087936 | tf_op jit(solution)/shard_map/convert_element_type | solution.py:73
  80.4 14.0 %convolution_convert_fusion = bf16[512,4096]{1,0:T(8,128)(2,1)} fusion(bf16[4096,2048]{1,0:T(8,128)(2,1)} %bitcast.93, s32[2048]{0:T(1024)S(1)} %eq.48), kind=kOutput, calls=%fused_computation.6 | convolution fusion | flops 8593080320 | bytes 20979712 | tf_op jit(solution)/shard_map/dot_general | solution.py:19
  94.4 5.5 %convolution_convert_fusion.3 = bf16[512,512]{0,1:T(8,128)(2,1)} fusion(bf16[512,4096]{1,0:T(8,128)(2,1)} %convolution_convert_fusion, bf16[4096,512]{1,0:T(8,128)(2,1)S(1)} %bitcast.96), kind=kOutput, calls=%fused_computation.23 | convolution fusion | flops 2147745792 | bytes 8912896 | tf_op jit(solution)/shard_map/dot_general | solution.py:19
  99.9 4.1 %all-to-all-start.2 = ((bf16[4,512,128]{1,2,0:T(8,128)(2,1)}), bf16[4,512,128]{1,2,0:T(8,128)(2,1)S(1)}, u32[]{:S(2)}, u32[]{:S(2)}) async-start(bf16[4,512,128]{1,2,0:T(8,128)(2,1)} %bitcast.51), calls=%async_computation.2 | async-start | bytes 1048576 | tf_op jit(solution)/shard_map/all_to_all | solution.py:23
  105.6 8.2 %all-to-all-done.2 = bf16[4,512,128]{1,2,0:T(8,128)(2,1)S(1)} async-done(((bf16[4,512,128]{1,2,0:T(8,128)(2,1)}), bf16[4,512,128]{1,2,0:T(8,128)(2,1)S(1)}, u32[]{:S(2)}, u32[]{:S(2)}) %all-to-all-start.2) | async-done | bytes 524320 | tf_op jit(solution)/shard_map/all_to_all | solution.py:23
  114.3 13.4 %all_gather.15 = bf16[512,512]{0,1:T(8,128)(2,1)S(1)} all-gather(bf16[512,128]{0,1:T(8,128)(2,1)S(1)} %get-tuple-element.57), channel_id=1, replica_groups=mesh['rel'=4,'ent'=32] {'rel'}, dimensions={1}, use_global_device_ids=true | all-gather | bytes 655360 | tf_op jit(solution)/shard_map/all_gather | solution.py:89
  127.8 4.5 %convolution_convert_fusion.2.clone.5 = bf16[4096,512]{1,0:T(8,128)(2,1)S(1)} fusion(bf16[4096,512]{1,0:T(8,128)(2,1)} %bitcast.95, bf16[512,512]{0,1:T(8,128)(2,1)S(1)} %all_gather.15, f32[512]{0:T(512)S(1)} %maximum_divide_fusion), kind=kOutput, calls=%fused_computation.8.clone.clone.clone.2 | convolution fusion | flops 2150367232 | bytes 8914944 | tf_op jit(solution)/shard_map/dot_general | solution.py:19
  132.3 14.6 %fusion.3 = f32[4096,2048]{1,0:T(8,128)} fusion(s32[2048]{0:T(1024)S(1)} %eq.48, bf16[4096,512]{1,0:T(8,128)(2,1)S(1)} %convolution_convert_fusion.2.clone.5), kind=kOutput, calls=%fused_computation.14 | convolution fusion | flops 8590983168 | bytes 37756928 | tf_op jit(solution)/shard_map/dot_general | solution.py:19
  146.9 12.5 %multiply_reduce_fusion = bf16[128,2048]{1,0:T(8,128)(2,1)S(1)} fusion(f32[32,128,2048]{2,1,0:T(8,128)} %bitcast.92, f32[32,2048]{1,0:T(8,128)S(1)} %fusion.7), kind=kLoop, calls=%fused_computation.1 | loop fusion | flops 16515072 | bytes 34340864 | tf_op jit(solution)/shard_map/reduce_sum | solution.py:103
  160.4 7.4 %all-to-all-start.3 = ((bf16[32,64,128]{2,1,0:T(8,128)(2,1)}), bf16[32,64,128]{2,1,0:T(8,128)(2,1)S(1)}, u32[]{:S(2)}, u32[]{:S(2)}) async-start(bf16[32,64,128]{2,1,0:T(8,128)(2,1)} %bitcast.54), calls=%async_computation.3 | async-start | bytes 1048576 | tf_op jit(solution)/shard_map/all_to_all | solution.py:23
  167.8 6.5 %convolution_convert_fusion.1 = bf16[4096,512]{1,0:T(8,128)(2,1)} fusion(bf16[512,4096]{1,0:T(8,128)(2,1)} %convolution_convert_fusion, bf16[512,512]{0,1:T(8,128)(2,1)S(1)} %all_gather.15, f32[512]{0:T(512)S(1)} %maximum_divide_fusion), kind=kOutput, calls=%fused_computation.7 | convolution fusion | flops 2150367232 | bytes 8914944 | tf_op jit(solution)/shard_map/dot_general | solution.py:19
  176.3 8.0 %all-to-all-start.5 = ((bf16[32,128,512]{2,1,0:T(8,128)(2,1)}), bf16[32,128,512]{2,1,0:T(8,128)(2,1)}, u32[]{:S(2)}, u32[]{:S(2)}) async-start(bf16[32,128,512]{2,1,0:T(8,128)(2,1)} %bitcast.97), calls=%async_computation.5 | async-start | bytes 8388608 | tf_op jit(solution)/shard_map/all_to_all | solution.py:23
  185.5 49.0 %all-to-all-done.5 = bf16[32,128,512]{2,1,0:T(8,128)(2,1)} async-done(((bf16[32,128,512]{2,1,0:T(8,128)(2,1)}), bf16[32,128,512]{2,1,0:T(8,128)(2,1)}, u32[]{:S(2)}, u32[]{:S(2)}) %all-to-all-start.5) | async-done | bytes 4194336 | tf_op jit(solution)/shard_map/all_to_all | solution.py:23
  235.4 3.5 %all-to-all-start.4 = ((bf16[512,4,128]{2,0,1:T(8,128)(2,1)}), bf16[512,4,128]{2,0,1:T(8,128)(2,1)S(1)}, u32[]{:S(2)}, u32[]{:S(2)}) async-start(bf16[512,4,128]{2,0,1:T(8,128)(2,1)} %tile.2), calls=%async_computation.4 | async-start | bytes 1048576 | tf_op jit(solution)/shard_map/all_to_all | solution.py:13
  241.7 6.3 %collective-permute-start = (f32[128,512]{1,0:T(8,128)S(1)}, f32[128,512]{1,0:T(8,128)S(1)}, u32[]{:S(2)}, u32[]{:S(2)}) collective-permute-start(f32[128,512]{1,0:T(8,128)S(1)} %convert_reduce_fusion), channel_id=1, source_target_pairs={{0,0},{1,4},{2,8},{3,12},{4,16},{5,20},{6,24},{7,28},{8,32},{9,36}... | collective-permute-start | bytes 786440 | tf_op jit(solution)/shard_map/ppermute | solution.py:100
  248.0 17.9 %all_gather.14 = bf16[512,512]{0,1:T(8,128)(2,1)S(1)} all-gather(bf16[512,128]{0,1:T(8,128)(2,1)S(1)} %get-tuple-element.58), channel_id=1, replica_groups=mesh['rel'=4,'ent'=32] {'rel'}, dimensions={1}, use_global_device_ids=true | all-gather | bytes 655360 | tf_op jit(solution)/shard_map/all_gather | solution.py:88
  (56 shorter events, 26.6 us)
Async XLA Ops:
  0.6 52.4 %copy-start = (bf16[512,512]{1,0:T(8,128)(2,1)S(1)}, bf16[512,512]{1,0:T(8,128)(2,1)}, u32[]{:S(2)}) copy-start(bf16[512,512]{1,0:T(8,128)(2,1)} %param.12) | copy-start | bytes 1572868
  45.5 11.8 %all-to-all-start = ((s32[32,1,128]{2,1,0:T(1,128)}), s32[32,1,128]{2,1,0:T(1,128)S(1)}, u32[]{:S(2)}, u32[]{:S(2)}) async-start(s32[32,1,128]{2,1,0:T(1,128)} %reshape.372), calls=%async_computation | async-start | bytes 32768 | tf_op jit(solution)/shard_map/all_to_all | solution.py:23
  57.3 15.9 %all-to-all-start.1 = ((bf16[32,64,128]{2,1,0:T(8,128)(2,1)}), bf16[32,64,128]{2,1,0:T(8,128)(2,1)S(1)}, u32[]{:S(2)}, u32[]{:S(2)}) async-start(bf16[32,64,128]{2,1,0:T(8,128)(2,1)} %bitcast.44), calls=%async_computation.1 | async-start | bytes 1048576 | tf_op jit(solution)/shard_map/all_to_all | solution.py:23
  64.0 6.2 %copy-start.4 = (f32[1000,32]{0,1:T(8,128)S(1)}, f32[1000,32]{0,1:T(8,128)}, u32[]{:S(2)}) copy-start(f32[1000,32]{0,1:T(8,128)} %param.15) | copy-start | bytes 384004
  80.4 14.0 %copy-start.2 = (bf16[32,128,512]{2,1,0:T(8,128)(2,1)S(1)}, bf16[32,128,512]{2,1,0:T(8,128)(2,1)}, u32[]{:S(2)}) copy-start(bf16[32,128,512]{2,1,0:T(8,128)(2,1)} %constant_dynamic-slice_fusion.1) | copy-start | bytes 12582916
  94.4 19.5 %copy-start.3 = (bf16[512,512]{1,0:T(8,128)(2,1)S(1)}, bf16[512,512]{1,0:T(8,128)(2,1)}, u32[]{:S(2)}) copy-start(bf16[512,512]{1,0:T(8,128)(2,1)} %param.13) | copy-start | bytes 1572868
  99.9 13.9 %all-to-all-start.2 = ((bf16[4,512,128]{1,2,0:T(8,128)(2,1)}), bf16[4,512,128]{1,2,0:T(8,128)(2,1)S(1)}, u32[]{:S(2)}, u32[]{:S(2)}) async-start(bf16[4,512,128]{1,2,0:T(8,128)(2,1)} %bitcast.51), calls=%async_computation.2 | async-start | bytes 1048576 | tf_op jit(solution)/shard_map/all_to_all | solution.py:23
  160.4 16.0 %all-to-all-start.3 = ((bf16[32,64,128]{2,1,0:T(8,128)(2,1)}), bf16[32,64,128]{2,1,0:T(8,128)(2,1)S(1)}, u32[]{:S(2)}, u32[]{:S(2)}) async-start(bf16[32,64,128]{2,1,0:T(8,128)(2,1)} %bitcast.54), calls=%async_computation.3 | async-start | bytes 1048576 | tf_op jit(solution)/shard_map/all_to_all | solution.py:23
  176.3 58.2 %all-to-all-start.5 = ((bf16[32,128,512]{2,1,0:T(8,128)(2,1)}), bf16[32,128,512]{2,1,0:T(8,128)(2,1)}, u32[]{:S(2)}, u32[]{:S(2)}) async-start(bf16[32,128,512]{2,1,0:T(8,128)(2,1)} %bitcast.97), calls=%async_computation.5 | async-start | bytes 8388608 | tf_op jit(solution)/shard_map/all_to_all | solution.py:23
  235.4 31.6 %all-to-all-start.4 = ((bf16[512,4,128]{2,0,1:T(8,128)(2,1)}), bf16[512,4,128]{2,0,1:T(8,128)(2,1)S(1)}, u32[]{:S(2)}, u32[]{:S(2)}) async-start(bf16[512,4,128]{2,0,1:T(8,128)(2,1)} %tile.2), calls=%async_computation.4 | async-start | bytes 1048576 | tf_op jit(solution)/shard_map/all_to_all | solution.py:13
  238.9 30.0 %copy-start.1 = (bf16[512,512]{1,0:T(8,128)(2,1)S(1)}, bf16[512,512]{1,0:T(8,128)(2,1)}, u32[]{:S(2)}) copy-start(bf16[512,512]{1,0:T(8,128)(2,1)} %param.12) | copy-start | bytes 1572868
  241.7 26.5 %collective-permute-start = (f32[128,512]{1,0:T(8,128)S(1)}, f32[128,512]{1,0:T(8,128)S(1)}, u32[]{:S(2)}, u32[]{:S(2)}) collective-permute-start(f32[128,512]{1,0:T(8,128)S(1)} %convert_reduce_fusion), channel_id=1, source_target_pairs={{0,0},{1,4},{2,8},{3,12},{4,16},{5,20},{6,24},{7,28},{8,32},{9,36}... | collective-permute-start | bytes 786440 | tf_op jit(solution)/shard_map/ppermute | solution.py:100
